TPU v7x, 32 devices: a whole 2x2x4 slice. The times are simulated.
32 devices in a mesh: grp: 2 (over x), seq: 16 (over z, y, core).
Axes of the slice: x: 2, y: 2, z: 4, core: 2. Of those that a mesh axis runs over, the one named last changes fastest.
Arguments:
- queries: bfloat16 [16384, 2048], P(('grp', 'seq')), parts along dimension 0, may hold values from -16 to 16
- key_rows: bfloat16 [16384, 2048], P(('grp', 'seq')), parts along dimension 0, may hold values from -4 to 4
- value_rows: bfloat16 [16384, 2048], P(('grp', 'seq')), parts along dimension 0, may hold values from -6 to 6
- box_bins: int32 [2, 16384], P(None, ('grp', 'seq')), parts along dimension 1, may hold values from 0 to 255
- slopes: float32 [16], replicated, may hold values from 0.05 to 3
- near_lists: int32 [128, 5], P('grp'), parts along dimension 0, may hold values from -1 to 59, as said below
Outputs:
- attended: bfloat16 [16384, 2048], P(('grp', 'seq')), parts along dimension 0
There are 2 independent parts, one for each index of `grp`. A program takes and returns all parts, laid end to end along the dimension named above; an argument that names none is the same for every part. Nothing has to cross between parts.
Inputs may be any that keep to these rules, and one draw needn't show every extreme that they name: `near_lists`: block ids lie on one of the 6 devices before the query block's device, the device of block c being c // 4; the ids listed for one query block differ from one another; the lists of one device's 4 query blocks together name exactly 2 distinct blocks of each of those preceding devices that exist, and -1 stands for the blocks of devices before the first.
All inputs are finite; a program needn't handle non-finite values.
Results may differ from a plain program's by a relative error of at most 0.0038.
Values may be sent and summed in bfloat16 or wider, within the bound.
A program may use at most 128 MiB of HBM per device.

v0:
```python
import math

import jax
import jax.numpy as jnp
from jax import lax
from jax.sharding import PartitionSpec as P

BLOCK = 128
REACH = 6


def shifted(shard, axis, by):
    peers = lax.axis_size(axis)
    pairs = [(i, i + by) for i in range(peers) if 0 <= i + by < peers]
    return lax.ppermute(shard, axis, pairs)


def attend(query_block, all_keys, all_values, query_bins, key_bins, present, slopes):
    row_count, features = query_block.shape
    head_count = slopes.shape[0]
    head_dim = features // head_count
    key_count = all_keys.shape[0]
    products = jnp.einsum(
        "qhd,khd->hqk",
        query_block.reshape(row_count, head_count, head_dim),
        all_keys.reshape(key_count, head_count, head_dim),
        preferred_element_type=jnp.float32,
    )
    query_spot = query_bins.astype(jnp.float32)
    key_spot = key_bins.astype(jnp.float32)
    spread = jnp.abs(query_spot[0][:, None] - key_spot[0][None, :]) + jnp.abs(
        query_spot[1][:, None] - key_spot[1][None, :]
    )
    scores = (
        products * (1.0 / math.sqrt(head_dim)) - slopes[:, None, None] * (spread * 0.015625)[None]
    )
    row_ids = jnp.arange(row_count, dtype=jnp.int32)[:, None]
    col_ids = jnp.arange(key_count, dtype=jnp.int32)[None, :]
    listed = jnp.concatenate([jnp.ones((row_count,), bool), jnp.repeat(present, row_count)])[
        None, :
    ]
    allowed = jnp.where(col_ids < row_count, col_ids <= row_ids, listed)
    masked = jnp.where(allowed[None], scores, -jnp.inf)
    largest = jnp.max(masked, axis=2, keepdims=True)
    exponent = jnp.exp(masked - largest)
    totals = jnp.sum(exponent, axis=2)
    weights = exponent.astype(jnp.bfloat16)
    mixture = jnp.einsum(
        "hqk,khd->qhd",
        weights,
        all_values.reshape(key_count, head_count, head_dim),
        preferred_element_type=jnp.float32,
    )
    return (
        (mixture / jnp.transpose(totals)[:, :, None])
        .reshape(row_count, features)
        .astype(jnp.bfloat16)
    )


def body(queries, key_rows, value_rows, box_bins, slopes, near_lists):
    token_count, features = queries.shape
    blocks = token_count // BLOCK
    device = lax.axis_index("seq")
    query_blocks = queries.reshape(blocks, BLOCK, features)
    key_blocks = key_rows.reshape(blocks, BLOCK, features)
    value_blocks = value_rows.reshape(blocks, BLOCK, features)
    own_bins = jnp.transpose(box_bins.reshape(2, blocks, BLOCK), (1, 0, 2))
    every_bins = lax.all_gather(box_bins, "seq", axis=1, tiled=True)
    all_bins = jnp.transpose(every_bins.reshape(2, -1, BLOCK), (1, 0, 2))
    own_lists = lax.dynamic_slice_in_dim(near_lists, device * blocks, blocks, 0)
    present = own_lists >= 0
    clamped = jnp.maximum(own_lists, 0)
    distance = device - clamped // blocks
    block_slot = clamped % blocks
    arrivals = [shifted((key_rows, value_rows), "seq", offset) for offset in range(1, REACH + 1)]
    window_keys = jnp.stack([arrived[0] for arrived in arrivals]).reshape(
        REACH * blocks, BLOCK, features
    )
    window_values = jnp.stack([arrived[1] for arrived in arrivals]).reshape(
        REACH * blocks, BLOCK, features
    )
    slot_index = (distance - 1) * blocks + block_slot
    slot_index = jnp.where(present, slot_index, 0)

    def one_block(inputs):
        query_block, own_keys, own_values, query_bins, slots, listed_ids, listed_present = inputs
        all_keys = jnp.concatenate(
            [own_keys[None], jnp.take(window_keys, slots, axis=0)], 0
        ).reshape(-1, features)
        all_values = jnp.concatenate(
            [own_values[None], jnp.take(window_values, slots, axis=0)], 0
        ).reshape(-1, features)
        key_bins = jnp.concatenate([query_bins[None], jnp.take(all_bins, listed_ids, axis=0)], 0)
        key_bins = jnp.transpose(key_bins, (1, 0, 2)).reshape(2, -1)
        return attend(
            query_block, all_keys, all_values, query_bins, key_bins, listed_present, slopes
        )

    results = lax.map(
        one_block, (query_blocks, key_blocks, value_blocks, own_bins, slot_index, clamped, present)
    )
    return results.reshape(token_count, features)


def solution(mesh):
    placed = (
        P(("grp", "seq"), None),
        P(("grp", "seq"), None),
        P(("grp", "seq"), None),
        P(None, ("grp", "seq")),
        P(),
        P("grp", None),
    )
    return jax.shard_map(
        body, mesh=mesh, in_specs=placed, out_specs=P(("grp", "seq"), None), check_vma=False
    )
```

profile of v0, /device:TPU:25, one launch (start us, length us, event | category | flops | bytes accessed | tf_op | source)
XLA Modules:
  0.0 809.9 jit_solution(5328308519130120279)
XLA Ops:
  0.0 3.8 collective-permute-start
  10.5 183.5 %all_gather.3 = s32[2,8192]{1,0:T(2,128)S(1)} all-gather(s32[2,512]{1,0:T(2,128)} %param.13), channel_id=1, replica_groups=mesh['grp'=2,'seq'=16] {'seq'}, dimensions={1}, use_global_device_ids=true | all-gather | bytes 69632 | tf_op jit(solution)/shard_map/all_gather | solution.py:69
  208.9 35.9 %collective-permute-done.4 = bf16[512,2048]{1,0:T(8,128)(2,1)S(1)} collective-permute-done((bf16[512,2048]{1,0:T(8,128)(2,1)}, bf16[512,2048]{1,0:T(8,128)(2,1)S(1)}, u32[]{:S(2)}, u32[]{:S(2)}) %collective-permute-start.4) | collective-permute-done | bytes 2097184 | tf_op jit(solution)/shard_map/ppermute | solution.py:15
  246.4 111.8 %collective-permute-done.5 = bf16[512,2048]{1,0:T(8,128)(2,1)S(1)} collective-permute-done((bf16[512,2048]{1,0:T(8,128)(2,1)}, bf16[512,2048]{1,0:T(8,128)(2,1)S(1)}, u32[]{:S(2)}, u32[]{:S(2)}) %collective-permute-start.5) | collective-permute-done | bytes 2097184 | tf_op jit(solution)/shard_map/ppermute | solution.py:15
  360.1 35.5 %collective-permute-done.8 = bf16[512,2048]{1,0:T(8,128)(2,1)S(1)} collective-permute-done((bf16[512,2048]{1,0:T(8,128)(2,1)S(1)}, bf16[512,2048]{1,0:T(8,128)(2,1)S(1)}, u32[]{:S(2)}, u32[]{:S(2)}) %collective-permute-start.8) | collective-permute-done | bytes 2097184 | tf_op jit(solution)/shard_map/ppermute | solution.py:15
  396.4 252.1 %collective-permute-done.11 = bf16[512,2048]{1,0:T(8,128)(2,1)S(1)} collective-permute-done((bf16[512,2048]{1,0:T(8,128)(2,1)S(1)}, bf16[512,2048]{1,0:T(8,128)(2,1)S(1)}, u32[]{:S(2)}, u32[]{:S(2)}) %collective-permute-start.11) | collective-permute-done | bytes 2097184 | tf_op jit(solution)/shard_map/ppermute | solution.py:15
  648.8 4.5 copy-done.2
  653.2 155.9 %while.10 = (s32[]{:T(128)}, bf16[4,128,2048]{2,1,0:T(8,128)(2,1)}, bf16[4,128,2048]{2,1,0:T(8,128)(2,1)}, s32[4,5]{1,0:T(4,128)S(1)}, bf16[24,128,2048]{2,1,0:T...) while((s32[]{:T(128)}, bf16[4,128,2048]{2,1,0:T(8,128)(2,1)}, ...), condition=%wide.region_3.5_spmd, body=%wide.region_0.4_spmd.sunk | while | flops 839126336 | bytes 81245688 | solution.py:100
  654.8 7.1 gather_fusion.2
  661.9 7.0 gather_fusion.1
  677.4 5.3 fusion.55
  687.3 3.9 divide_convert_fusion.2
  693.8 7.1 gather_fusion.2
  700.9 7.0 gather_fusion.1
  716.4 5.3 fusion.55
  726.3 3.9 divide_convert_fusion.2
  732.8 7.1 gather_fusion.2
  739.9 7.0 gather_fusion.1
  755.4 5.3 fusion.55
  765.2 3.9 divide_convert_fusion.2
  771.8 7.1 gather_fusion.2
  778.8 7.0 gather_fusion.1
  794.4 5.3 fusion.55
  804.2 3.9 divide_convert_fusion.2
  (178 shorter events, 88.9 us)
Async XLA Ops:
  0.0 10.3 %copy-start = (s32[64,5]{0,1:T(8,128)S(1)}, s32[64,5]{0,1:T(8,128)}, u32[]{:S(2)}) copy-start(s32[64,5]{0,1:T(8,128)} %param.15) | copy-start | bytes 3844
  0.0 194.5 %collective-permute-start = (bf16[512,2048]{1,0:T(8,128)(2,1)}, bf16[512,2048]{1,0:T(8,128)(2,1)}, u32[]{:S(2)}, u32[]{:S(2)}) collective-permute-start(bf16[512,2048]{1,0:T(8,128)(2,1)} %param.12), channel_id=1, source_target_pairs={{0,1},{1,2},{2,3},{3,4},{4,5},{5,6},{6,7},{7,8},{8,9},{9,10},{10,1... | collective-permute-start | bytes 6291464 | tf_op jit(solution)/shard_map/ppermute | solution.py:15
  3.8 193.7 %collective-permute-start.6 = (bf16[512,2048]{1,0:T(8,128)(2,1)}, bf16[512,2048]{1,0:T(8,128)(2,1)}, u32[]{:S(2)}, u32[]{:S(2)}) collective-permute-start(bf16[512,2048]{1,0:T(8,128)(2,1)} %param.11), channel_id=1, source_target_pairs={{0,1},{1,2},{2,3},{3,4},{4,5},{5,6},{6,7},{7,8},{8,9},{9,10},{10,1... | collective-permute-start | bytes 6291464 | tf_op jit(solution)/shard_map/ppermute | solution.py:15
  5.8 195.0 %collective-permute-start.1 = (bf16[512,2048]{1,0:T(8,128)(2,1)}, bf16[512,2048]{1,0:T(8,128)(2,1)}, u32[]{:S(2)}, u32[]{:S(2)}) collective-permute-start(bf16[512,2048]{1,0:T(8,128)(2,1)} %param.12), channel_id=1, source_target_pairs={{0,2},{1,3},{2,4},{3,5},{4,6},{5,7},{6,8},{7,9},{8,10},{9,11},{10,... | collective-permute-start | bytes 6291464 | tf_op jit(solution)/shard_map/ppermute | solution.py:15
  7.7 196.7 %collective-permute-start.2 = (bf16[512,2048]{1,0:T(8,128)(2,1)}, bf16[512,2048]{1,0:T(8,128)(2,1)}, u32[]{:S(2)}, u32[]{:S(2)}) collective-permute-start(bf16[512,2048]{1,0:T(8,128)(2,1)} %param.12), channel_id=1, source_target_pairs={{0,3},{1,4},{2,5},{3,6},{4,7},{5,8},{6,9},{7,10},{8,11},{9,12},{10... | collective-permute-start | bytes 6291464 | tf_op jit(solution)/shard_map/ppermute | solution.py:15
  9.0 198.5 %collective-permute-start.3 = (bf16[512,2048]{1,0:T(8,128)(2,1)}, bf16[512,2048]{1,0:T(8,128)(2,1)S(1)}, u32[]{:S(2)}, u32[]{:S(2)}) collective-permute-start(bf16[512,2048]{1,0:T(8,128)(2,1)} %param.12), channel_id=1, source_target_pairs={{0,4},{1,5},{2,6},{3,7},{4,8},{5,9},{6,10},{7,11},{8,12},{9,13},{1... | collective-permute-start | bytes 6291464 | tf_op jit(solution)/shard_map/ppermute | solution.py:15
  194.5 50.3 %collective-permute-start.4 = (bf16[512,2048]{1,0:T(8,128)(2,1)}, bf16[512,2048]{1,0:T(8,128)(2,1)S(1)}, u32[]{:S(2)}, u32[]{:S(2)}) collective-permute-start(bf16[512,2048]{1,0:T(8,128)(2,1)} %param.12), channel_id=1, source_target_pairs={{0,5},{1,6},{2,7},{3,8},{4,9},{5,10},{6,11},{7,12},{8,13},{9,14},{... | collective-permute-start | bytes 6291464 | tf_op jit(solution)/shard_map/ppermute | solution.py:15
  197.6 160.6 %collective-permute-start.5 = (bf16[512,2048]{1,0:T(8,128)(2,1)}, bf16[512,2048]{1,0:T(8,128)(2,1)S(1)}, u32[]{:S(2)}, u32[]{:S(2)}) collective-permute-start(bf16[512,2048]{1,0:T(8,128)(2,1)} %param.12), channel_id=1, source_target_pairs={{0,6},{1,7},{2,8},{3,9},{4,10},{5,11},{6,12},{7,13},{8,14},{9,15},... | collective-permute-start | bytes 6291464 | tf_op jit(solution)/shard_map/ppermute | solution.py:15
  200.7 159.1 %collective-permute-start.7 = (bf16[512,2048]{1,0:T(8,128)(2,1)S(1)}, bf16[512,2048]{1,0:T(8,128)(2,1)S(1)}, u32[]{:S(2)}, u32[]{:S(2)}) collective-permute-start(bf16[512,2048]{1,0:T(8,128)(2,1)S(1)} %copy-done.4), channel_id=1, source_target_pairs={{0,2},{1,3},{2,4},{3,5},{4,6},{5,7},{6,8},{7,9},{8,10},{9,11},{10,... | collective-permute-start | bytes 6291464 | tf_op jit(solution)/shard_map/ppermute | solution.py:15
  204.4 191.2 %collective-permute-start.8 = (bf16[512,2048]{1,0:T(8,128)(2,1)S(1)}, bf16[512,2048]{1,0:T(8,128)(2,1)S(1)}, u32[]{:S(2)}, u32[]{:S(2)}) collective-permute-start(bf16[512,2048]{1,0:T(8,128)(2,1)S(1)} %copy-done.4), channel_id=1, source_target_pairs={{0,3},{1,4},{2,5},{3,6},{4,7},{5,8},{6,9},{7,10},{8,11},{9,12},{10... | collective-permute-start | bytes 6291464 | tf_op jit(solution)/shard_map/ppermute | solution.py:15
  207.5 188.4 %collective-permute-start.9 = (bf16[512,2048]{1,0:T(8,128)(2,1)S(1)}, bf16[512,2048]{1,0:T(8,128)(2,1)S(1)}, u32[]{:S(2)}, u32[]{:S(2)}) collective-permute-start(bf16[512,2048]{1,0:T(8,128)(2,1)S(1)} %copy-done.4), channel_id=1, source_target_pairs={{0,4},{1,5},{2,6},{3,7},{4,8},{5,9},{6,10},{7,11},{8,12},{9,13},{1... | collective-permute-start | bytes 6291464 | tf_op jit(solution)/shard_map/ppermute | solution.py:15
  244.8 151.3 %collective-permute-start.10 = (bf16[512,2048]{1,0:T(8,128)(2,1)S(1)}, bf16[512,2048]{1,0:T(8,128)(2,1)S(1)}, u32[]{:S(2)}, u32[]{:S(2)}) collective-permute-start(bf16[512,2048]{1,0:T(8,128)(2,1)S(1)} %copy-done.4), channel_id=1, source_target_pairs={{0,5},{1,6},{2,7},{3,8},{4,9},{5,10},{6,11},{7,12},{8,13},{9,14},{... | collective-permute-start | bytes 6291464 | tf_op jit(solution)/shard_map/ppermute | solution.py:15
  358.2 290.3 %collective-permute-start.11 = (bf16[512,2048]{1,0:T(8,128)(2,1)S(1)}, bf16[512,2048]{1,0:T(8,128)(2,1)S(1)}, u32[]{:S(2)}, u32[]{:S(2)}) collective-permute-start(bf16[512,2048]{1,0:T(8,128)(2,1)S(1)} %copy-done.4), channel_id=1, source_target_pairs={{0,6},{1,7},{2,8},{3,9},{4,10},{5,11},{6,12},{7,13},{8,14},{9,15},... | collective-permute-start | bytes 6291464 | tf_op jit(solution)/shard_map/ppermute | solution.py:15
  359.9 288.9 %copy-start.3 = (bf16[6,512,2048]{2,1,0:T(8,128)(2,1)}, bf16[6,512,2048]{2,1,0:T(8,128)(2,1)S(1)}, u32[]{:S(2)}) copy-start(bf16[6,512,2048]{2,1,0:T(8,128)(2,1)S(1)} %bitcast_dynamic-update-slice_fusion.6) | copy-start | bytes 37748740
  396.4 256.9 %copy-start.7 = (f32[16]{0:T(128)S(1)}, f32[16]{0:T(128)}, u32[]{:S(2)}) copy-start(f32[16]{0:T(128)} %param.14) | copy-start | bytes 196
  648.7 4.5 copy-start.2
  653.2 15.7 %copy-start.5 = (s32[64,2,128]{2,1,0:T(2,128)}, s32[64,2,128]{2,1,0:T(2,128)S(1)}, u32[]{:S(2)}) copy-start(s32[64,2,128]{2,1,0:T(2,128)S(1)} %get-tuple-element.282) | copy-start | bytes 196612 | tf_op jit(solution)/shard_map/while
  687.3 5.0 copy-start.6
  692.2 15.7 %copy-start.5 = (s32[64,2,128]{2,1,0:T(2,128)}, s32[64,2,128]{2,1,0:T(2,128)S(1)}, u32[]{:S(2)}) copy-start(s32[64,2,128]{2,1,0:T(2,128)S(1)} %get-tuple-element.282) | copy-start | bytes 196612 | tf_op jit(solution)/shard_map/while
  726.2 5.0 copy-start.6
  731.2 15.7 %copy-start.5 = (s32[64,2,128]{2,1,0:T(2,128)}, s32[64,2,128]{2,1,0:T(2,128)S(1)}, u32[]{:S(2)}) copy-start(s32[64,2,128]{2,1,0:T(2,128)S(1)} %get-tuple-element.282) | copy-start | bytes 196612 | tf_op jit(solution)/shard_map/while
  765.2 5.0 copy-start.6
  770.2 15.7 %copy-start.5 = (s32[64,2,128]{2,1,0:T(2,128)}, s32[64,2,128]{2,1,0:T(2,128)S(1)}, u32[]{:S(2)}) copy-start(s32[64,2,128]{2,1,0:T(2,128)S(1)} %get-tuple-element.282) | copy-start | bytes 196612 | tf_op jit(solution)/shard_map/while
  804.2 5.0 copy-start.6
  (6 other events, 18.9 us)
where the time goes:
time: 811 us; the launch traced here: 810 us
  waiting for transfers between devices  435 us (54%)
  blocking collectives  184 us (23%)
  local copies, waits for them, and re-layouts  106 us (13%)
  matrix products  36.7 us (5%)
  other arithmetic  27.4 us (3%)
  starting transfers between devices  20.2 us (2%)
    ppermute x12, waiting for transfers between devices, shifted(): return lax.ppermute(shard, axis, pairs)  435 us
    all_gather x1, blocking collectives, body(): every_bins = lax.all_gather(box_bins, 'seq', axis=1, tiled=True)  184 us
    gather x4, local copies, waits for them, and re-layouts, one_block(): jnp.take(window_keys, slots, axis=0)  28.2 us
    gather x4, local copies, waits for them, and re-layouts, one_block(): jnp.take(window_values, slots, axis=0)  28 us
    dot_general x4, matrix products, attend(): jnp.einsum('qhd,khd->hqk', query_block.reshape(row_count, head_count, hea...  21.3 us
    ppermute x12, starting transfers between devices, shifted(): return lax.ppermute(shard, axis, pairs)  20.2 us
  transfers between devices with their start and end apart: 12, of which 4 were waited for; matrix products, arithmetic and copies ran while one was open for 1% of the time, Pallas kernels for 0%

commit v1 on v0

v1 whole, which is shorter than its diff:
```python
import functools
import math

import jax
import jax.numpy as jnp
from jax import lax
from jax.experimental import pallas as pl
from jax.experimental.pallas import tpu as pltpu
from jax.sharding import PartitionSpec as P

BLOCK = 128
REACH = 6
BLOCKS = 4
PIECES = 2 * BLOCKS
SPARE = 9 * BLOCKS
HIGH_ROAD = (0, 1)
LONG_ROAD = (0, 1, 2)


def exchange(n, k_ref, v_ref, bins_ref, wk_ref, wv_ref, wbins_ref, send_sems, recv_sems, bin_send, bin_recv, own_sems):
    me = lax.axis_index("seq")
    planes = n // 4
    a, b, c = me // 4, (me // 2) % 2, me % 2
    has_next, has_prev, has_prev2 = a < planes - 1, a >= 1, a >= 2
    up, across, beside = me + 4, me + 2 - 4 * b, me + 1 - 2 * c
    b0, b1, c0, c1 = b == 0, b == 1, c == 0, c == 1
    both = jnp.logical_and

    barrier = pltpu.get_barrier_semaphore()
    for d in range(1, REACH + 1):

        @pl.when(me >= d)
        def _():
            pl.semaphore_signal(barrier, inc=1, device_id={"seq": me - d}, device_id_type=pl.DeviceIdType.MESH)

        @pl.when(me + d < n)
        def _():
            pl.semaphore_signal(barrier, inc=1, device_id={"seq": me + d}, device_id_type=pl.DeviceIdType.MESH)

    pl.semaphore_wait(barrier, jnp.minimum(me, REACH) + jnp.minimum(n - 1 - me, REACH))

    def own(t):
        return (k_ref, v_ref)[t // BLOCKS].at[t % BLOCKS]

    def slot(index, t):
        return (wk_ref, wv_ref)[t // BLOCKS].at[index * BLOCKS + t % BLOCKS]

    sent = []

    def send(flow, t, source, index, target, cond):
        def copy():
            return pltpu.make_async_remote_copy(
                src_ref=own(t) if source is None else slot(source, t),
                dst_ref=slot(index, t),
                send_sem=send_sems.at[flow, t],
                recv_sem=recv_sems.at[index, t],
                device_id={"seq": target},
                device_id_type=pl.DeviceIdType.MESH,
            )

        @pl.when(cond)
        def _():
            copy().start()

        sent.append((copy, cond))

    def arrive(index, t, cond):
        @pl.when(cond)
        def _():
            pltpu.make_async_remote_copy(
                src_ref=slot(index, t),
                dst_ref=slot(index, t),
                send_sem=send_sems.at[0, t],
                recv_sem=recv_sems.at[index, t],
                device_id={"seq": beside},
                device_id_type=pl.DeviceIdType.MESH,
            ).wait_recv()

    def bin_copy(d, device):
        return pltpu.make_async_remote_copy(
            src_ref=bins_ref,
            dst_ref=wbins_ref.at[d - 1],
            send_sem=bin_send.at[d - 1],
            recv_sem=bin_recv.at[d - 1],
            device_id={"seq": device},
            device_id_type=pl.DeviceIdType.MESH,
        )

    for d in range(1, REACH + 1):

        @pl.when(me + d < n)
        def _():
            bin_copy(d, me + d).start()

    for t in range(PIECES):
        send(0, t, None, 3 + 2 * b + c, up, has_next)
        send(1, t, None, c, across, b0)
        send(2, t, None, 2 * b, beside, c0)
    spares = [
        pltpu.make_async_copy(own(0), wk_ref.at[SPARE], own_sems.at[0]),
        pltpu.make_async_copy(own(BLOCKS), wv_ref.at[SPARE], own_sems.at[1]),
    ]
    for spare in spares:
        spare.start()

    two_up = both(has_prev, has_next)
    for t in range(PIECES):
        arrive(3 + 2 * b + c, t, has_prev)
        send(3, t, 3 + 2 * b + c, 3 + 2 * b + c, beside, has_prev)
        if t in LONG_ROAD:
            send(4, t, 3 + 2 * b + c, 3 + 2 * b + c, across, both(has_prev, b1))
        else:
            send(4, t, 3 + 2 * b + c, 3 + 2 * b + c, across, has_prev)
        if t in HIGH_ROAD:
            send(5, t, 5 + c, 7 + c, up, both(two_up, b1))
        arrive(c, t, b1)
        send(6, t, c, c, beside, b1)
        if t in LONG_ROAD:
            send(7, t, c, 3 + c, up, both(has_next, b1))
        arrive(5 + c, t, both(has_prev, b0))
        send(6, t, 5 + c, 5 + c, beside, both(has_prev, b0))
        if t not in HIGH_ROAD:
            send(5, t, 5 + c, 7 + c, up, both(two_up, b0))
    for t in HIGH_ROAD:
        arrive(7 + c, t, both(has_prev2, b1))
        send(8, t, 7 + c, 7 + c, across, both(has_prev2, b1))
    for t in list(LONG_ROAD) + [t for t in range(PIECES) if t not in LONG_ROAD]:
        arrive(3 + c, t, both(has_prev, b1))
        send(9, t, 3 + c, 3 + c, beside, both(has_prev, both(b1, c1)))
    for t in [t for t in range(PIECES) if t not in HIGH_ROAD] + list(HIGH_ROAD):
        arrive(7 + c, t, both(has_prev2, b0))
        send(9, t, 7 + c, 7 + c, beside, both(has_prev2, both(b0, c1)))

    for t in range(PIECES):
        arrive(2 * b, t, c1)
        arrive(4 + 2 * b - c, t, has_prev)
        arrive(1 - c, t, b1)
        arrive(6 - c, t, both(has_prev, b0))
        arrive(4, t, both(has_prev, both(b1, c0)))
        arrive(8, t, both(has_prev2, both(b0, c0)))
    for d in range(1, REACH + 1):

        @pl.when(me >= d)
        def _():
            bin_copy(d, me).wait_recv()

    for copy, cond in sent:

        @pl.when(cond)
        def _(copy=copy):
            copy().wait_send()

    for d in range(1, REACH + 1):

        @pl.when(me + d < n)
        def _():
            bin_copy(d, me + d).wait_send()

    for spare in spares:
        spare.wait()


def attend(near, heads, places_ref, bin_places_ref, slopes_ref, q_ref, k_ref, v_ref, bins_ref, wbins_ref, *rest):
    key_refs = (k_ref,) + rest[:near]
    value_refs = (v_ref,) + rest[near : 2 * near]
    out_ref, bias = rest[2 * near :]
    block = pl.program_id(0)
    own = bins_ref[block].astype(jnp.float32)
    rows_x = jnp.transpose(jnp.broadcast_to(own[0:1], (BLOCK, BLOCK)))
    rows_y = jnp.transpose(jnp.broadcast_to(own[1:2], (BLOCK, BLOCK)))
    row_ids = lax.broadcasted_iota(jnp.int32, (BLOCK, BLOCK), 0)
    col_ids = lax.broadcasted_iota(jnp.int32, (BLOCK, BLOCK), 1)
    for j in range(near + 1):
        if j == 0:
            spots, allowed = own, col_ids <= row_ids
        else:
            place = bin_places_ref[block, j - 1]
            spots = wbins_ref[jnp.maximum(place, 0)].astype(jnp.float32)
            allowed = (col_ids * 0 + place) >= 0
        spread = jnp.abs(rows_x - spots[0:1]) + jnp.abs(rows_y - spots[1:2])
        bias[:, j * BLOCK : (j + 1) * BLOCK] = jnp.where(allowed, spread * 0.015625, jnp.inf)
    dim = q_ref.shape[-1] // heads
    factor = math.log2(math.e)
    for h in range(heads):
        cols = slice(h * dim, (h + 1) * dim)
        query = q_ref[0, :, cols]
        keys = jnp.concatenate([ref[0, :, cols] for ref in key_refs], 0)
        values = jnp.concatenate([ref[0, :, cols] for ref in value_refs], 0)
        products = lax.dot_general(query, keys, (((1,), (1,)), ((), ())), preferred_element_type=jnp.float32)
        scores = products * (factor / math.sqrt(dim)) - (slopes_ref[h] * factor) * bias[...]
        largest = jnp.max(scores, axis=1, keepdims=True)
        exponent = jnp.exp2(scores - largest)
        totals = jnp.sum(exponent, axis=1, keepdims=True)
        mixture = jnp.dot(exponent.astype(jnp.bfloat16), values, preferred_element_type=jnp.float32)
        out_ref[0, :, cols] = (mixture / totals).astype(jnp.bfloat16)


def body(n, queries, key_rows, value_rows, box_bins, slopes, near_lists):
    token_count, features = queries.shape
    blocks = token_count // BLOCK
    near = near_lists.shape[1]
    heads = slopes.shape[0]
    device = lax.axis_index("seq")
    shape = (blocks, BLOCK, features)
    queries, key_rows, value_rows = (x.reshape(shape) for x in (queries, key_rows, value_rows))
    bins = jnp.transpose(box_bins.reshape(2, blocks, BLOCK), (1, 0, 2))
    lists = lax.dynamic_slice_in_dim(near_lists, device * blocks, blocks, 0)
    source, inside = lists // blocks, lists % blocks
    index = source % 4 + jnp.array([0, 3, 5], jnp.int32)[jnp.clip(device // 4 - source // 4, 0, 2)]
    places = jnp.where(lists >= 0, index * blocks + inside, SPARE)
    bin_places = jnp.where(lists >= 0, (device - source - 1) * blocks + inside, -1)

    anywhere = pl.BlockSpec(memory_space=pl.ANY)
    wk, wv, wbins = pl.pallas_call(
        functools.partial(exchange, n),
        out_shape=(
            jax.ShapeDtypeStruct((SPARE + 1, BLOCK, features), key_rows.dtype),
            jax.ShapeDtypeStruct((SPARE + 1, BLOCK, features), value_rows.dtype),
            jax.ShapeDtypeStruct((REACH, blocks, 2, BLOCK), jnp.int32),
        ),
        in_specs=[anywhere] * 3,
        out_specs=(anywhere,) * 3,
        scratch_shapes=[
            pltpu.SemaphoreType.DMA((10, PIECES)),
            pltpu.SemaphoreType.DMA((9, PIECES)),
            pltpu.SemaphoreType.DMA((REACH,)),
            pltpu.SemaphoreType.DMA((REACH,)),
            pltpu.SemaphoreType.DMA((2,)),
        ],
        compiler_params=pltpu.CompilerParams(collective_id=0, has_side_effects=True),
        name="exchange",
    )(key_rows, value_rows, bins)

    tile = (1, BLOCK, features)
    mine = pl.BlockSpec(tile, lambda i, *_: (i, 0, 0))
    listed = [pl.BlockSpec(tile, lambda i, places, *_, j=j: (places[i, j], 0, 0)) for j in range(near)]
    whole = pl.BlockSpec(memory_space=pltpu.VMEM)
    out = pl.pallas_call(
        functools.partial(attend, near, heads),
        grid_spec=pltpu.PrefetchScalarGridSpec(
            num_scalar_prefetch=3,
            grid=(blocks,),
            in_specs=[mine, mine, mine, whole, whole] + listed + listed,
            out_specs=mine,
            scratch_shapes=[pltpu.VMEM((BLOCK, (near + 1) * BLOCK), jnp.float32)],
        ),
        out_shape=jax.ShapeDtypeStruct(shape, jnp.bfloat16),
        compiler_params=pltpu.CompilerParams(vmem_limit_bytes=48 << 20),
        name="attend",
    )(places, bin_places, slopes, queries, key_rows, value_rows, bins, wbins.reshape(REACH * blocks, 2, BLOCK), *([wk] * near), *([wv] * near))
    return out.reshape(token_count, features)


def solution(mesh):
    placed = (
        P(("grp", "seq"), None),
        P(("grp", "seq"), None),
        P(("grp", "seq"), None),
        P(None, ("grp", "seq")),
        P(),
        P("grp", None),
    )
    return jax.shard_map(
        functools.partial(body, mesh.shape["seq"]),
        mesh=mesh,
        in_specs=placed,
        out_specs=P(("grp", "seq"), None),
        check_vma=False,
    )
```

time: 811 us -> 198 us (0.24)
  waiting for transfers between devices: 435 us -> 0 us
  Pallas kernels: 0 us -> 193 us
  blocking collectives: 184 us -> 0 us
  local copies, waits for them, and re-layouts: 106 us -> 4.72 us
  matrix products: 36.7 us -> 0 us
  other arithmetic: 27.4 us -> 0.06 us
  starting transfers between devices: 20.2 us -> 0 us
    ppermute x12 -> x0, waiting for transfers between devices: 435 us -> none  [shifted(): return lax.ppermute(shard, axis, pairs)]
    pallas_call x0 -> x2, Pallas kernels: none -> 193 us  [the longest x1 167 us: body(): pl.pallas_call(functools.partial(exchange, n), out_shape=(jax.ShapeDtypeS...]
    all_gather x1 -> x0, blocking collectives: 184 us -> none  [body(): every_bins = lax.all_gather(box_bins, 'seq', axis=1, tiled=True)]
    gather x12 -> x2, local copies, waits for them, and re-layouts: 58.6 us -> 1.44 us  [body(): jnp.array([0, 3, 5], jnp.int32)[jnp.clip(device // 4 - source // 4, 0, 2)]]
    dot_general x8 -> x0, matrix products: 36.7 us -> none  [the longest x4 21.3 us: attend(): jnp.einsum('qhd,khd->hqk', query_block.reshape(row_count, head_count, hea...]
    ppermute x12 -> x0, starting transfers between devices: 20.2 us -> none  [shifted(): return lax.ppermute(shard, axis, pairs)]
    while x32 -> x0, local copies, waits for them, and re-layouts: 15 us -> none
    dynamic_slice x13 -> x1, local copies, waits for them, and re-layouts: 13.5 us -> 0.07 us  [body(): lists = lax.dynamic_slice_in_dim(near_lists, device * blocks, blocks, 0)]
  transfers between devices with their start and end apart: 12 -> 0, of which waited for: 4 -> 0; matrix products, arithmetic and copies ran while one was open for 1% -> 0% of each run, Pallas kernels for 0% -> 0%
where the time goes in v1:
time: 198 us
  Pallas kernels  193 us (97%)
  local copies, waits for them, and re-layouts  4.72 us (2%)
    pallas_call x1, Pallas kernels, body(): pl.pallas_call(functools.partial(exchange, n), out_shape=(jax.ShapeDtypeS...  167 us
    pallas_call x1, Pallas kernels, body(): pl.pallas_call(functools.partial(attend, near, heads), grid_spec=pltpu.Pr...  26.2 us

profile of v1, /device:TPU:25, one launch (start us, length us, event | category | flops | bytes accessed | tf_op | source)
XLA Modules:
  0.0 197.7 jit_solution(2642872517907623654)
XLA Ops:
  0.0 0.0 copy-start
  0.0 0.7 copy-done
  0.7 0.1 constant_dynamic-slice_fusion
  0.8 0.1 copy.10
  0.9 0.1 reshape.26
  1.0 1.4 gather_fusion
  2.3 0.1 reshape.25
  2.4 0.0 copy-start.1
  2.5 0.0 copy-start.4
  2.5 0.0 copy-start.5
  2.5 166.7 %exchange.1 = (bf16[37,128,2048]{2,1,0:T(8,128)(2,1)}, bf16[37,128,2048]{2,1,0:T(8,128)(2,1)}, s32[6,4,2,128]{3,2,1,0:T(2,128)}) custom-call(bf16[4,128,2048]{2,1,0:T(8,128)(2,1)} %bitcast.8, bf16[4,128,2048]{2,1,0:T(8,128)(2,1)} %bitcast.14, s32[4,2,128]{2,1,0:T(2,128)} %bitcast.12), custom_call_target="tpu_custom_call" | custom-call | tf_op jit(solution)/shard_map/exchange/pallas_call | solution.py:214
  169.2 0.0 copy-done.1
  169.2 0.0 copy-done.4
  169.2 0.0 copy-done.5
  169.2 0.0 copy-start.2
  169.2 1.6 copy-done.2
  170.8 0.0 copy-start.3
  170.8 0.7 copy-done.3
  171.5 26.2 %attend.1 = bf16[4,128,2048]{2,1,0:T(8,128)(2,1)} custom-call(s32[4,5]{1,0:T(4,128)S(1)} %fusion.3.places_ref, s32[4,5]{1,0:T(4,128)S(1)} %get-tuple-element.11.bin_places_ref, f32[16]{0:T(128)S(1)} %copy-done.5, bf16[4,128,2048]{2,1,0:T(8,128)(2,1)S(1)} %bitcast.10, bf16[4,128,2048]{2,1,0:T(8,128)(2,1)S(1)} %bitcast.9, bf16[4,128,2048]{2,1,0:T(8,128)(2,1)} %bitcast.15, ...), custom_call_target="tpu_custom_call" | custom-call | tf_op jit(solution)/shard_map/attend/pallas_call | solution.py:238
  (3 shorter events, 0.1 us)
Async XLA Ops:
  0.0 0.7 copy-start
  2.4 166.7 %copy-start.1 = (bf16[512,2048]{1,0:T(8,128)(2,1)S(1)}, bf16[512,2048]{1,0:T(8,128)(2,1)}, u32[]{:S(2)}) copy-start(bf16[512,2048]{1,0:T(8,128)(2,1)} %param.8) | copy-start | bytes 6291460
  2.5 166.7 %copy-start.4 = (s32[2,512]{1,0:T(2,128)S(1)}, s32[2,512]{1,0:T(2,128)}, u32[]{:S(2)}) copy-start(s32[2,512]{1,0:T(2,128)} %param.10) | copy-start | bytes 12292
  2.5 166.7 %copy-start.5 = (f32[16]{0:T(128)S(1)}, f32[16]{0:T(128)}, u32[]{:S(2)}) copy-start(f32[16]{0:T(128)} %slopes_ref.1) | copy-start | bytes 196
  169.2 1.6 copy-start.2
  170.8 0.7 copy-start.3

commit v2 on v1

--- a/solution.py
+++ b/solution.py
@@ -14,7 +14,8 @@
 PIECES = 2 * BLOCKS
 SPARE = 9 * BLOCKS
 HIGH_ROAD = (0, 1)
-LONG_ROAD = (0, 1, 2)
+ORDER = (0, 1, 4, 5, 2, 3, 6, 7)
+LONG_ROAD = (0, 1)
 
 
 def exchange(n, k_ref, v_ref, bins_ref, wk_ref, wv_ref, wbins_ref, send_sems, recv_sems, bin_send, bin_recv, own_sems):
@@ -25,6 +26,10 @@
     up, across, beside = me + 4, me + 2 - 4 * b, me + 1 - 2 * c
     b0, b1, c0, c1 = b == 0, b == 1, c == 0, c == 1
     both = jnp.logical_and
+
+    def kept(t, cond):
+        return cond if t % BLOCKS < 2 else both(cond, c1)
+
 
     barrier = pltpu.get_barrier_semaphore()
     for d in range(1, REACH + 1):
@@ -92,7 +97,7 @@
         def _():
             bin_copy(d, me + d).start()
 
-    for t in range(PIECES):
+    for t in ORDER:
         send(0, t, None, 3 + 2 * b + c, up, has_next)
         send(1, t, None, c, across, b0)
         send(2, t, None, 2 * b, beside, c0)
@@ -104,13 +109,13 @@
         spare.start()
 
     two_up = both(has_prev, has_next)
-    for t in range(PIECES):
+    for t in ORDER:
         arrive(3 + 2 * b + c, t, has_prev)
         send(3, t, 3 + 2 * b + c, 3 + 2 * b + c, beside, has_prev)
         if t in LONG_ROAD:
             send(4, t, 3 + 2 * b + c, 3 + 2 * b + c, across, both(has_prev, b1))
         else:
-            send(4, t, 3 + 2 * b + c, 3 + 2 * b + c, across, has_prev)
+            send(4, t, 3 + 2 * b + c, 3 + 2 * b + c, across, both(has_prev, jnp.logical_or(b1, kept(t, b0))))
         if t in HIGH_ROAD:
             send(5, t, 5 + c, 7 + c, up, both(two_up, b1))
         arrive(c, t, b1)
@@ -120,18 +125,18 @@
         arrive(5 + c, t, both(has_prev, b0))
         send(6, t, 5 + c, 5 + c, beside, both(has_prev, b0))
         if t not in HIGH_ROAD:
-            send(5, t, 5 + c, 7 + c, up, both(two_up, b0))
+            send(5, t, 5 + c, 7 + c, up, kept(t, both(two_up, b0)))
     for t in HIGH_ROAD:
         arrive(7 + c, t, both(has_prev2, b1))
         send(8, t, 7 + c, 7 + c, across, both(has_prev2, b1))
-    for t in list(LONG_ROAD) + [t for t in range(PIECES) if t not in LONG_ROAD]:
-        arrive(3 + c, t, both(has_prev, b1))
+    for t in ORDER:
+        arrive(3 + c, t, kept(t, both(has_prev, b1)))
         send(9, t, 3 + c, 3 + c, beside, both(has_prev, both(b1, c1)))
-    for t in [t for t in range(PIECES) if t not in HIGH_ROAD] + list(HIGH_ROAD):
-        arrive(7 + c, t, both(has_prev2, b0))
+    for t in [t for t in ORDER if t not in HIGH_ROAD] + list(HIGH_ROAD):
+        arrive(7 + c, t, kept(t, both(has_prev2, b0)))
         send(9, t, 7 + c, 7 + c, beside, both(has_prev2, both(b0, c1)))
 
-    for t in range(PIECES):
+    for t in ORDER:
         arrive(2 * b, t, c1)
         arrive(4 + 2 * b - c, t, has_prev)
         arrive(1 - c, t, b1)
@@ -158,6 +163,11 @@
 
     for spare in spares:
         spare.wait()
+
+
+def reorder(places_ref, k_ref, v_ref, k_out, v_out):
+    k_out[...] = k_ref[...]
+    v_out[...] = v_ref[...]
 
 
 def attend(near, heads, places_ref, bin_places_ref, slopes_ref, q_ref, k_ref, v_ref, bins_ref, wbins_ref, *rest):
@@ -207,8 +217,31 @@
     lists = lax.dynamic_slice_in_dim(near_lists, device * blocks, blocks, 0)
     source, inside = lists // blocks, lists % blocks
     index = source % 4 + jnp.array([0, 3, 5], jnp.int32)[jnp.clip(device // 4 - source // 4, 0, 2)]
-    places = jnp.where(lists >= 0, index * blocks + inside, SPARE)
+    block_ids = jnp.arange(n * blocks, dtype=jnp.int32).reshape(n, blocks)
+    far_lists = jnp.pad(near_lists.reshape(n, -1), ((0, REACH), (0, 0)), constant_values=-1)[REACH:]
+    first = jnp.any(far_lists[:, None, :] == block_ids[:, :, None], axis=2)
+    ahead = jnp.logical_or(
+        jnp.logical_and(first[:, None, :], jnp.logical_not(first)[:, :, None]),
+        jnp.logical_and(first[:, None, :] == first[:, :, None], jnp.tri(blocks, k=-1, dtype=bool)[None]),
+    )
+    order = jnp.sum(ahead.astype(jnp.int32), axis=2)
+    same = jnp.maximum(lists, 0)[:, :, None] == block_ids.reshape(-1)
+    inside_sent = jnp.sum(jnp.where(same, order.reshape(-1), 0), axis=2)
+    places = jnp.where(lists >= 0, index * blocks + inside_sent, SPARE)
+    own_order = lax.dynamic_slice_in_dim(order, device, 1, 0)[0]
     bin_places = jnp.where(lists >= 0, (device - source - 1) * blocks + inside, -1)
+
+    tile = (1, BLOCK, features)
+    mine = pl.BlockSpec(tile, lambda i, *_: (i, 0, 0))
+    moved = pl.BlockSpec(tile, lambda i, places: (places[i], 0, 0))
+    sent_keys, sent_values = pl.pallas_call(
+        reorder,
+        grid_spec=pltpu.PrefetchScalarGridSpec(
+            num_scalar_prefetch=1, grid=(blocks,), in_specs=[mine, mine], out_specs=(moved, moved)
+        ),
+        out_shape=(jax.ShapeDtypeStruct(shape, key_rows.dtype), jax.ShapeDtypeStruct(shape, value_rows.dtype)),
+        name="reorder",
+    )(own_order, key_rows, value_rows)
 
     anywhere = pl.BlockSpec(memory_space=pl.ANY)
     wk, wv, wbins = pl.pallas_call(
@@ -229,10 +262,8 @@
         ],
         compiler_params=pltpu.CompilerParams(collective_id=0, has_side_effects=True),
         name="exchange",
-    )(key_rows, value_rows, bins)
-
-    tile = (1, BLOCK, features)
-    mine = pl.BlockSpec(tile, lambda i, *_: (i, 0, 0))
+    )(sent_keys, sent_values, bins)
+
     listed = [pl.BlockSpec(tile, lambda i, places, *_, j=j: (places[i, j], 0, 0)) for j in range(near)]
     whole = pl.BlockSpec(memory_space=pltpu.VMEM)
     out = pl.pallas_call(

time: 198 us -> 186 us (0.939); the launches traced: 198 us -> 183 us
  Pallas kernels: 193 us -> 176 us
    pallas_call x1, Pallas kernels: 167 us -> 145 us  [body(): pl.pallas_call(functools.partial(exchange, n), out_shape=(jax.ShapeDtypeS...]
    pallas_call x0 -> x1, Pallas kernels: none -> 5.39 us  [body(): pl.pallas_call(reorder, grid_spec=pltpu.PrefetchScalarGridSpec(num_scalar...]
where the time goes in v2:
time: 186 us; the launch traced here: 183 us
  Pallas kernels  176 us (95%)
  local copies, waits for them, and re-layouts  5.85 us (3%)
    pallas_call x1, Pallas kernels, body(): pl.pallas_call(functools.partial(exchange, n), out_shape=(jax.ShapeDtypeS...  145 us
    pallas_call x1, Pallas kernels, body(): pl.pallas_call(functools.partial(attend, near, heads), grid_spec=pltpu.Pr...  26.1 us
    pallas_call x1, Pallas kernels, body(): pl.pallas_call(reorder, grid_spec=pltpu.PrefetchScalarGridSpec(num_scalar...  5.39 us

profile of v2, /device:TPU:25, one launch (start us, length us, event | category | flops | bytes accessed | tf_op | source)
XLA Modules:
  0.0 182.9 jit_solution(14200697313438623847)
XLA Ops:
  0.0 0.1 iota_compare_fusion.1
  0.1 0.8 copy.16
  0.9 0.1 reshape.64
  1.0 1.4 gather_fusion
  2.3 0.1 reshape.63
  2.4 0.1 copy.17
  2.5 0.1 reshape.54
  2.6 0.2 compare_reduce_fusion
  2.8 0.1 convert_reduce_fusion
  2.9 0.8 dynamic-slice_reduce_fusion.places_ref
  3.7 0.1 copy.19
  3.8 0.1 reshape.55
  3.9 0.2 select_reduce_fusion
  4.1 0.1 copy.20
  4.3 5.4 %reorder.1 = (bf16[4,128,2048]{2,1,0:T(8,128)(2,1)}, bf16[4,128,2048]{2,1,0:T(8,128)(2,1)}) custom-call(s32[4]{0:T(128)} %dynamic-slice_reduce_fusion.places_ref, bf16[4,128,2048]{2,1,0:T(8,128)(2,1)} %bitcast.8, bf16[4,128,2048]{2,1,0:T(8,128)(2,1)} %bitcast.14), custom_call_target="tpu_custom_call" | custom-call | tf_op jit(solution)/shard_map/reorder/pallas_call | solution.py:237
  9.7 0.0 copy-start
  9.7 144.8 %exchange.1 = (bf16[37,128,2048]{2,1,0:T(8,128)(2,1)}, bf16[37,128,2048]{2,1,0:T(8,128)(2,1)}, s32[6,4,2,128]{3,2,1,0:T(2,128)}) custom-call(bf16[4,128,2048]{2,1,0:T(8,128)(2,1)} %get-tuple-element.10.k_ref, bf16[4,128,2048]{2,1,0:T(8,128)(2,1)} %get-tuple-element.11.v_ref, s32[4,2,128]{2,1,0:T(2,128)} %bitcast.12), custom_call_target="tpu_custom_call" | custom-call | tf_op jit(solution)/shard_map/exchange/pallas_call | solution.py:247
  154.4 0.0 copy-done
  154.4 0.0 copy-done.3
  154.4 0.0 copy-done.4
  154.5 0.0 copy-start.1
  154.5 1.6 copy-done.1
  156.1 0.7 copy-done.2
  156.8 26.1 %attend.1 = bf16[4,128,2048]{2,1,0:T(8,128)(2,1)} custom-call(s32[4,5]{1,0:T(4,128)S(1)} %fusion.3.places_ref, s32[4,5]{1,0:T(4,128)S(1)} %get-tuple-element.15.bin_places_ref, f32[16]{0:T(128)S(1)} %copy-done.4, bf16[4,128,2048]{2,1,0:T(8,128)(2,1)S(1)} %bitcast.10, bf16[4,128,2048]{2,1,0:T(8,128)(2,1)S(1)} %bitcast.9, bf16[4,128,2048]{2,1,0:T(8,128)(2,1)} %bitcast.15, ...), custom_call_target="tpu_custom_call" | custom-call | tf_op jit(solution)/shard_map/attend/pallas_call | solution.py:269
  (10 shorter events, 0.1 us)
Async XLA Ops:
  9.7 144.8 %copy-start = (bf16[512,2048]{1,0:T(8,128)(2,1)S(1)}, bf16[512,2048]{1,0:T(8,128)(2,1)}, u32[]{:S(2)}) copy-start(bf16[512,2048]{1,0:T(8,128)(2,1)} %param.8) | copy-start | bytes 6291460
  9.7 144.8 %copy-start.3 = (s32[2,512]{1,0:T(2,128)S(1)}, s32[2,512]{1,0:T(2,128)}, u32[]{:S(2)}) copy-start(s32[2,512]{1,0:T(2,128)} %param.10) | copy-start | bytes 12292
  9.7 144.8 %copy-start.4 = (f32[16]{0:T(128)S(1)}, f32[16]{0:T(128)}, u32[]{:S(2)}) copy-start(f32[16]{0:T(128)} %slopes_ref.1) | copy-start | bytes 196
  154.5 1.6 copy-start.1
  156.0 0.7 copy-start.2
